TPU v7x, 32 devices: a whole 2x2x4 slice. The times are simulated.
32 devices in a mesh: grp: 2 (over x), samp: 16 (over z, y, core).
Axes of the slice: x: 2, y: 2, z: 4, core: 2. Of those that a mesh axis runs over, the one named last changes fastest.
Arguments:
- genotypes: int32 [32768, 2048], P(('grp', 'samp')), parts along dimension 0, may hold values from 0 to 2
- probe_signs: int32 [32, 32768], P(None, ('grp', 'samp')), parts along dimension 1, may hold values from 0 to 1
- phenotype: float32 [32768], P(('grp', 'samp')), parts along dimension 0, may hold values from -6 to 6
- marker_mean: float32 [2048], replicated, may hold values from 0.2 to 1.8
- marker_scale: float32 [2048], replicated, may hold values from 0.5 to 4
- marker_bin: int32 [2048], replicated, may hold values from 0 to 15, as said below
Outputs:
- products: float32 [16, 33, 32768], P(None, None, ('grp', 'samp')), parts along dimension 2
- gram: float32 [32, 16, 33], P('grp'), parts along dimension 0
There are 2 independent parts, one for each index of `grp`. A program takes and returns all parts, laid end to end along the dimension named above; an argument that names none is the same for every part. Nothing has to cross between parts.
Inputs may be any that keep to these rules, and one draw needn't show every extreme that they name: `marker_bin`: every bin holds exactly 128 markers.
All inputs are finite; a program needn't handle non-finite values.
Results may differ from a plain program's by a relative error of at most 0.0001.
Values sent between devices are 32-bit elements; how exact they have to be, the bound alone decides.
A program may use at most 128 MiB of HBM per device.

v0:
```python
import jax
import jax.numpy as jnp
from jax import lax
from jax.sharding import PartitionSpec as P

BINS = 16
M_BIN = 128


def shards(genotypes, probe_signs, phenotype, marker_mean, marker_scale, marker_bin):
    samples = genotypes.shape[0]
    devices = lax.axis_size("samp")
    total = jnp.float32(samples * devices)
    order = jnp.argsort(marker_bin, stable=True)
    picked = jnp.take(genotypes, order, axis=1).astype(jnp.float32)
    standard = (picked - marker_mean[order]) * marker_scale[order]
    vectors = jnp.concatenate(
        [(2 * probe_signs - 1).astype(jnp.float32), phenotype[None, :]], axis=0
    )
    share = lax.psum_scatter(
        jnp.dot(
            standard.T,
            vectors.T,
            precision=lax.Precision.HIGHEST,
            preferred_element_type=jnp.float32,
        ),
        "samp",
        scatter_dimension=0,
        tiled=True,
    )
    scores = lax.all_gather(share, "samp", axis=0, tiled=True)
    scores = scores / jnp.sqrt(total)
    blocks = standard.reshape(samples, BINS, M_BIN)
    weights = scores.reshape(BINS, M_BIN, scores.shape[1])
    products = jnp.einsum(
        "skm,kmr->krs", blocks, weights, precision=lax.Precision.HIGHEST
    ) / jnp.sqrt(jnp.float32(M_BIN))
    local_gram = jnp.einsum("krs,lrs->klr", products, products, precision=lax.Precision.HIGHEST)
    gram = lax.psum(local_gram, "samp") / total
    return (products, gram)


def solution(mesh):
    in_specs = (
        P(("grp", "samp"), None),
        P(None, ("grp", "samp")),
        P(("grp", "samp")),
        P(),
        P(),
        P(),
    )
    out_specs = (P(None, None, ("grp", "samp")), P("grp", None, None))
    return jax.shard_map(shards, mesh=mesh, in_specs=in_specs, out_specs=out_specs, check_vma=False)
```

profile of v0, /device:TPU:0, one launch (start us, length us, event | category | flops | bytes accessed | tf_op | source)
XLA Modules:
  0.0 233.8 jit_solution(9177498620670587703)
XLA Ops:
  7.2 0.0 copy-start
  7.2 0.0 copy-start.1
  7.2 0.0 reduce-scatter.2.cloned.1.call-start
  7.2 5.7 %sort.17 = (s32[2048]{0:T(1024)}, s32[2048]{0:T(1024)S(1)}) sort(s32[2048]{0:T(1024)} %param.11, s32[2048]{0:T(1024)S(1)} %iota.4), dimensions={0}, to_apply=%region_0.0 | sort | flops 22528 | bytes 32768 | tf_op jit(solution)/shard_map/jit(argsort)/sort | solution.py:14
  13.0 0.0 copy-done
  13.0 0.0 copy-start.3
  13.0 11.8 %gather_fusion.2 = f32[2048]{0:T(1024)S(1)} fusion(f32[2048]{0:T(1024)S(1)} %copy-done, s32[2048]{0:T(1024)S(1)} %fusion.25), kind=kCustom, calls=%fused_computation.2 | custom fusion | bytes 24576 | tf_op jit(solution)/shard_map/gather | solution.py:16
  24.8 0.0 copy-done.1
  24.8 11.8 %gather_fusion.1 = f32[2048]{0:T(1024)S(1)} fusion(f32[2048]{0:T(1024)S(1)} %copy-done.1, s32[2048]{0:T(1024)S(1)} %fusion.25), kind=kCustom, calls=%fused_computation.1 | custom fusion | bytes 24576 | tf_op jit(solution)/shard_map/gather | solution.py:16
  36.6 0.0 copy-done.3
  36.6 9.3 %copy.15 = s32[1024,2048]{0,1:T(8,128)} copy(s32[1024,2048]{1,0:T(8,128)} %param.6) | data formatting | bytes 16777216 | tf_op args[0]
  45.9 15.1 %gather_fusion = s32[2048,1024]{1,0:T(8,128)} fusion(s32[1024,2048]{0,1:T(8,128)} %copy.15, s32[2048]{0:T(1024)S(1)} %fusion.25), kind=kCustom, calls=%fused_computation | custom fusion | bytes 16785408 | tf_op jit(solution)/shard_map/jit(_take)/gather | solution.py:15
  61.1 12.3 %fusion.3 = f32[2048,33]{0,1:T(8,128)} fusion(s32[2048,1024]{1,0:T(8,128)} %gather_fusion, f32[2048]{0:T(1024)S(1)} %gather_fusion.2, f32[2048]{0:T(1024)S(1)} %gather_fusion.1, pred[2048]{0:T(1024)(128)(4,1)S(1)} %compare_and_fusion, f32[1,1024]{1,0:T(1,128)S(1)} %bitcast.31, f32[32,1024]{1,0:T(8,128)S(1)} %add_convert_fusion), kind=kOutput, calls=%fused_computation.7 | convolution fusion | flops 838894592 | bytes 8812544 | tf_op jit(solution)/shard_map/dot_general | solution.py:21
  73.3 0.0 reduce-scatter.2.cloned.1.call-update
  73.4 9.3 %copy.16 = s32[1024,16,128]{2,0,1:T(8,128)} copy(s32[1024,16,128]{0,2,1:T(8,128)} %bitcast.26) | data formatting | bytes 16777216 | tf_op jit(solution)/shard_map/jit(_take)/gather | solution.py:15
  82.6 45.9 %reduce-scatter.2.cloned.1.call-done = f32[128,33]{0,1:T(8,128)} async-done(((f32[2048,33]{0,1:T(8,128)}), f32[128,33]{0,1:T(8,128)}) %reduce-scatter.2.cloned.1.call-update) | async-done | bytes 16912 | tf_op jit(solution)/shard_map/reduce_scatter | solution.py:20
  128.6 20.7 %all_gather.3 = f32[2048,33]{0,1:T(8,128)S(1)} all-gather(f32[128,33]{0,1:T(8,128)} %reduce-scatter.2.cloned.1.call-done), channel_id=1, replica_groups=mesh['grp'=2,'samp'=16] {'samp'}, dimensions={0}, use_global_device_ids=true | all-gather | bytes 287232 | tf_op jit(solution)/shard_map/all_gather | solution.py:31
  149.3 0.1 copy.22
  149.4 11.3 %fusion.18 = f32[16,33,1024]{2,1,0:T(8,128)S(1)} fusion(s32[1024,16,128]{2,0,1:T(8,128)} %copy.16, f32[16,128]{1,0:T(8,128)S(1)} %bitcast.29, f32[16,128]{1,0:T(8,128)S(1)} %bitcast.30, pred[16,128]{1,0:T(8,128)(4,1)S(1)} %fusion.31, f32[16,128,33]{1,0,2:T(8,128)S(1)} %slice_bitcast_fusion), kind=kOutput, calls=%fused_computation.21 | convolution fusion | flops 839401472 | bytes 10840064 | tf_op jit(solution)/shard_map/skm,kmr->krs/dot_general | solution.py:35
  160.7 1.3 copy.20
  161.9 0.0 copy-start.2
  162.0 3.1 %convolution_bitcast_fusion = f32[16,16,33]{0,1,2:T(8,128)S(1)} fusion(f32[16,33,1024]{2,0,1:T(8,128)S(1)} %copy.20), kind=kOutput, calls=%fused_computation.22 | convolution fusion | flops 103809024 | bytes 2196480 | tf_op jit(solution)/shard_map/krs,lrs->klr/dot_general | solution.py:38
  165.1 61.0 %psum.7 = f32[16,16,33]{0,1,2:T(8,128)S(1)} all-reduce(f32[16,16,33]{0,1,2:T(8,128)S(1)} %convolution_bitcast_fusion), channel_id=1, replica_groups=mesh['grp'=2,'samp'=16] {'samp'}, use_global_device_ids=true, to_apply=%region_2.3 | all-reduce | flops 8448 | bytes 67584 | tf_op jit(solution)/shard_map/psum | solution.py:39
  226.1 0.8 copy.21
  (11 shorter events, 0.1 us)
Async XLA Ops:
  7.2 5.8 %copy-start = (f32[2048]{0:T(1024)S(1)}, f32[2048]{0:T(1024)}, u32[]{:S(2)}) copy-start(f32[2048]{0:T(1024)} %param.10) | copy-start | bytes 24580
  7.2 17.6 %copy-start.1 = (f32[2048]{0:T(1024)S(1)}, f32[2048]{0:T(1024)}, u32[]{:S(2)}) copy-start(f32[2048]{0:T(1024)} %param.9) | copy-start | bytes 24580
  7.2 121.4 %reduce-scatter.2.cloned.1.call-start = ((), (), s32[]{:S(2)}) async-start(), calls=%async_computation.1 | async-start | bytes 348160 | tf_op jit(solution)/shard_map/reduce_scatter | solution.py:20
  13.0 23.6 %copy-start.3 = (s32[32,1024]{1,0:T(8,128)S(1)}, s32[32,1024]{1,0:T(8,128)}, u32[]{:S(2)}) copy-start(s32[32,1024]{1,0:T(8,128)} %param.7) | copy-start | bytes 393220
  45.9 15.2 %copy-start.4 = (f32[1024]{0:T(1024)S(1)}, f32[1024]{0:T(1024)}, u32[]{:S(2)}) copy-start(f32[1024]{0:T(1024)} %param.8) | copy-start | bytes 12292
  161.9 65.0 %copy-start.2 = (f32[16,33,1024]{2,0,1:T(8,128)}, f32[16,33,1024]{2,0,1:T(8,128)S(1)}, u32[]{:S(2)}) copy-start(f32[16,33,1024]{2,0,1:T(8,128)S(1)} %copy.20) | copy-start | bytes 6488068
Sparse Core Ops, SparseCore 0:
  73.5 55.0 reduce-scatter.1
where the time goes:
time: 234 us
  blocking collectives  81.7 us (35%)
  local copies, waits for them, and re-layouts  59.5 us (25%)
  waiting for transfers between devices  45.9 us (20%)
  matrix products  26.7 us (11%)
  between operations  14.2 us (6%)
  other arithmetic  5.82 us (2%)
    psum x1, blocking collectives, shards(): gram = lax.psum(local_gram, 'samp') / total  61 us
    reduce_scatter x1, waiting for transfers between devices, shards(): lax.psum_scatter(jnp.dot(standard.T, vectors.T, precision=lax.Precision.H...  45.9 us
    gather x2, local copies, waits for them, and re-layouts, shards(): picked = jnp.take(genotypes, order, axis=1).astype(jnp.float32)  24.4 us
    gather x2, local copies, waits for them, and re-layouts, shards(): standard = (picked - marker_mean[order]) * marker_scale[order]  23.6 us
    all_gather x1, blocking collectives, shards(): scores = lax.all_gather(share, 'samp', axis=0, tiled=True)  20.7 us
    dot_general x1, matrix products, shards(): jnp.dot(standard.T, vectors.T, precision=lax.Precision.HIGHEST, preferred...  12.3 us
    unnamed x14, local copies, waits for them, and re-layouts  11.5 us
    dot_general x1, matrix products, shards(): jnp.einsum('skm,kmr->krs', blocks, weights, precision=lax.Precision.HIGHEST)  11.3 us
  transfers between devices with their start and end apart: 1, of which 1 were waited for; matrix products, arithmetic and copies ran while one was open for 4% of the time, Pallas kernels for 0%

commit v1 on v0

--- a/solution.py
+++ b/solution.py
@@ -28,7 +28,30 @@
         scatter_dimension=0,
         tiled=True,
     )
-    scores = lax.all_gather(share, "samp", axis=0, tiled=True)
+
+    def waves_pass(x0, where_dim):
+        mat_out = lax.psum(1, "samp")
+        right_arr = lax.axis_index("samp")
+        a_next, far_arr, e_now = (mat_out, right_arr, x0.shape[where_dim])
+        prior = range(a_next)
+        u_next = map(lambda b: (b, (b + 1) % a_next), prior)
+        inbox = list(u_next)
+        before = jnp.zeros(
+            (*x0.shape[:where_dim], a_next * e_now, *x0.shape[where_dim + 1 :]), x0.dtype
+        )
+        work_now = x0
+        m = 0
+        while m < a_next:
+            later = (far_arr - m) % a_next
+            before = lax.dynamic_update_slice_in_dim(
+                before, work_now, later * e_now, axis=where_dim
+            )
+            if m < a_next - 1:
+                work_now = lax.ppermute(work_now, "samp", inbox)
+            m += 1
+        return before
+
+    scores = waves_pass(share, 0)
     scores = scores / jnp.sqrt(total)
     blocks = standard.reshape(samples, BINS, M_BIN)
     weights = scores.reshape(BINS, M_BIN, scores.shape[1])

time: 234 us -> 302 us (1.29)
  waiting for transfers between devices: 45.9 us -> 134 us
  blocking collectives: 81.7 us -> 60.7 us
    ppermute x0 -> x15, waiting for transfers between devices: none -> 87.9 us  [waves_pass(): work_now = lax.ppermute(work_now, 'samp', inbox)]
    all_gather x1 -> x0, blocking collectives: 20.7 us -> none  [shards(): scores = lax.all_gather(share, 'samp', axis=0, tiled=True)]
  transfers between devices with their start and end apart: 1 -> 16, of which waited for: 1 -> 16; matrix products, arithmetic and copies ran while one was open for 4% -> 3% of each run, Pallas kernels for 0% -> 0%
where the time goes in v1:
time: 302 us
  waiting for transfers between devices  134 us (44%)
  blocking collectives  60.7 us (20%)
  local copies, waits for them, and re-layouts  60.2 us (20%)
  matrix products  26.7 us (9%)
  between operations  14.5 us (5%)
  other arithmetic  5.82 us (2%)
    ppermute x15, waiting for transfers between devices, waves_pass(): work_now = lax.ppermute(work_now, 'samp', inbox)  87.9 us
    psum x1, blocking collectives, shards(): gram = lax.psum(local_gram, 'samp') / total  60.7 us
    reduce_scatter x1, waiting for transfers between devices, shards(): lax.psum_scatter(jnp.dot(standard.T, vectors.T, precision=lax.Precision.H...  45.7 us
    gather x2, local copies, waits for them, and re-layouts, shards(): picked = jnp.take(genotypes, order, axis=1).astype(jnp.float32)  24.4 us
    gather x2, local copies, waits for them, and re-layouts, shards(): standard = (picked - marker_mean[order]) * marker_scale[order]  23.6 us
    dot_general x1, matrix products, shards(): jnp.dot(standard.T, vectors.T, precision=lax.Precision.HIGHEST, preferred...  12.3 us
    unnamed x14, local copies, waits for them, and re-layouts  11.4 us
    dot_general x1, matrix products, shards(): jnp.einsum('skm,kmr->krs', blocks, weights, precision=lax.Precision.HIGHEST)  11.3 us
  transfers between devices with their start and end apart: 16, of which 16 were waited for; matrix products, arithmetic and copies ran while one was open for 3% of the time, Pallas kernels for 0%

profile of v1, /device:TPU:0, one launch (start us, length us, event | category | flops | bytes accessed | tf_op | source)
XLA Modules:
  0.0 301.5 jit_solution(10872221180139865947)
XLA Ops:
  7.2 5.7 %sort.17 = (s32[2048]{0:T(1024)}, s32[2048]{0:T(1024)S(1)}) sort(s32[2048]{0:T(1024)} %param.11, s32[2048]{0:T(1024)S(1)} %iota.4), dimensions={0}, to_apply=%region_0.0 | sort | flops 22528 | bytes 32768 | tf_op jit(solution)/shard_map/jit(argsort)/sort | solution.py:14
  13.0 9.2 %copy.14 = s32[1024,2048]{0,1:T(8,128)} copy(s32[1024,2048]{1,0:T(8,128)} %param.6) | data formatting | bytes 16777216 | tf_op args[0]
  22.2 15.1 %gather_fusion = s32[2048,1024]{1,0:T(8,128)} fusion(s32[1024,2048]{0,1:T(8,128)} %copy.14, s32[2048]{0:T(1024)S(1)} %fusion.25), kind=kCustom, calls=%fused_computation | custom fusion | bytes 16785408 | tf_op jit(solution)/shard_map/jit(_take)/gather | solution.py:15
  37.4 11.8 %gather_fusion.1 = f32[2048]{0:T(1024)S(1)} fusion(f32[2048]{0:T(1024)S(1)} %copy-done, s32[2048]{0:T(1024)S(1)} %fusion.25), kind=kCustom, calls=%fused_computation.1 | custom fusion | bytes 24576 | tf_op jit(solution)/shard_map/gather | solution.py:16
  49.2 11.8 %gather_fusion.2 = f32[2048]{0:T(1024)S(1)} fusion(f32[2048]{0:T(1024)S(1)} %copy-done.1, s32[2048]{0:T(1024)S(1)} %fusion.25), kind=kCustom, calls=%fused_computation.2 | custom fusion | bytes 24576 | tf_op jit(solution)/shard_map/gather | solution.py:16
  61.0 12.3 %fusion.3 = f32[2048,33]{0,1:T(8,128)} fusion(s32[2048,1024]{1,0:T(8,128)} %gather_fusion, f32[2048]{0:T(1024)S(1)} %gather_fusion.2, f32[2048]{0:T(1024)S(1)} %gather_fusion.1, pred[2048]{0:T(1024)(128)(4,1)S(1)} %compare_and_fusion, f32[1,1024]{1,0:T(1,128)S(1)} %bitcast.31, f32[32,1024]{1,0:T(8,128)S(1)} %add_convert_fusion), kind=kOutput, calls=%fused_computation.7 | convolution fusion | flops 838894592 | bytes 8812544 | tf_op jit(solution)/shard_map/dot_general | solution.py:21
  73.6 9.2 %copy.15 = s32[1024,16,128]{2,0,1:T(8,128)} copy(s32[1024,16,128]{0,2,1:T(8,128)} %bitcast.26) | data formatting | bytes 16777216 | tf_op jit(solution)/shard_map/jit(_take)/gather | solution.py:15
  82.9 45.7 %reduce-scatter.2.cloned.1.call-done = f32[128,33]{0,1:T(8,128)} async-done(((f32[2048,33]{0,1:T(8,128)}), f32[128,33]{0,1:T(8,128)}) %reduce-scatter.2.cloned.1.call-update) | async-done | bytes 16912 | tf_op jit(solution)/shard_map/reduce_scatter | solution.py:20
  134.7 5.9 %collective-permute-done.1 = f32[128,33]{0,1:T(8,128)S(1)} collective-permute-done((f32[128,33]{0,1:T(8,128)S(1)}, f32[128,33]{0,1:T(8,128)S(1)}, u32[]{:S(2)}, u32[]{:S(2)}) %collective-permute-start.1) | collective-permute-done | bytes 16928 | tf_op jit(solution)/shard_map/ppermute | solution.py:50
  140.6 5.9 %collective-permute-done.2 = f32[128,33]{0,1:T(8,128)S(1)} collective-permute-done((f32[128,33]{0,1:T(8,128)S(1)}, f32[128,33]{0,1:T(8,128)S(1)}, u32[]{:S(2)}, u32[]{:S(2)}) %collective-permute-start.2) | collective-permute-done | bytes 16928 | tf_op jit(solution)/shard_map/ppermute | solution.py:50
  146.5 5.9 %collective-permute-done.3 = f32[128,33]{0,1:T(8,128)S(1)} collective-permute-done((f32[128,33]{0,1:T(8,128)S(1)}, f32[128,33]{0,1:T(8,128)S(1)}, u32[]{:S(2)}, u32[]{:S(2)}) %collective-permute-start.3) | collective-permute-done | bytes 16928 | tf_op jit(solution)/shard_map/ppermute | solution.py:50
  152.4 5.9 %collective-permute-done.4 = f32[128,33]{0,1:T(8,128)S(1)} collective-permute-done((f32[128,33]{0,1:T(8,128)S(1)}, f32[128,33]{0,1:T(8,128)S(1)}, u32[]{:S(2)}, u32[]{:S(2)}) %collective-permute-start.4) | collective-permute-done | bytes 16928 | tf_op jit(solution)/shard_map/ppermute | solution.py:50
  158.3 5.9 %collective-permute-done.5 = f32[128,33]{0,1:T(8,128)S(1)} collective-permute-done((f32[128,33]{0,1:T(8,128)S(1)}, f32[128,33]{0,1:T(8,128)S(1)}, u32[]{:S(2)}, u32[]{:S(2)}) %collective-permute-start.5) | collective-permute-done | bytes 16928 | tf_op jit(solution)/shard_map/ppermute | solution.py:50
  164.2 5.9 %collective-permute-done.6 = f32[128,33]{0,1:T(8,128)S(1)} collective-permute-done((f32[128,33]{0,1:T(8,128)S(1)}, f32[128,33]{0,1:T(8,128)S(1)}, u32[]{:S(2)}, u32[]{:S(2)}) %collective-permute-start.6) | collective-permute-done | bytes 16928 | tf_op jit(solution)/shard_map/ppermute | solution.py:50
  170.1 5.9 %collective-permute-done.7 = f32[128,33]{0,1:T(8,128)S(1)} collective-permute-done((f32[128,33]{0,1:T(8,128)S(1)}, f32[128,33]{0,1:T(8,128)S(1)}, u32[]{:S(2)}, u32[]{:S(2)}) %collective-permute-start.7) | collective-permute-done | bytes 16928 | tf_op jit(solution)/shard_map/ppermute | solution.py:50
  176.0 5.9 %collective-permute-done.8 = f32[128,33]{0,1:T(8,128)S(1)} collective-permute-done((f32[128,33]{0,1:T(8,128)S(1)}, f32[128,33]{0,1:T(8,128)S(1)}, u32[]{:S(2)}, u32[]{:S(2)}) %collective-permute-start.8) | collective-permute-done | bytes 16928 | tf_op jit(solution)/shard_map/ppermute | solution.py:50
  181.9 5.9 %collective-permute-done.9 = f32[128,33]{0,1:T(8,128)S(1)} collective-permute-done((f32[128,33]{0,1:T(8,128)S(1)}, f32[128,33]{0,1:T(8,128)S(1)}, u32[]{:S(2)}, u32[]{:S(2)}) %collective-permute-start.9) | collective-permute-done | bytes 16928 | tf_op jit(solution)/shard_map/ppermute | solution.py:50
  187.8 5.9 %collective-permute-done.10 = f32[128,33]{0,1:T(8,128)S(1)} collective-permute-done((f32[128,33]{0,1:T(8,128)S(1)}, f32[128,33]{0,1:T(8,128)S(1)}, u32[]{:S(2)}, u32[]{:S(2)}) %collective-permute-start.10) | collective-permute-done | bytes 16928 | tf_op jit(solution)/shard_map/ppermute | solution.py:50
  193.7 5.9 %collective-permute-done.11 = f32[128,33]{0,1:T(8,128)S(1)} collective-permute-done((f32[128,33]{0,1:T(8,128)S(1)}, f32[128,33]{0,1:T(8,128)S(1)}, u32[]{:S(2)}, u32[]{:S(2)}) %collective-permute-start.11) | collective-permute-done | bytes 16928 | tf_op jit(solution)/shard_map/ppermute | solution.py:50
  199.6 5.9 %collective-permute-done.12 = f32[128,33]{0,1:T(8,128)S(1)} collective-permute-done((f32[128,33]{0,1:T(8,128)S(1)}, f32[128,33]{0,1:T(8,128)S(1)}, u32[]{:S(2)}, u32[]{:S(2)}) %collective-permute-start.12) | collective-permute-done | bytes 16928 | tf_op jit(solution)/shard_map/ppermute | solution.py:50
  205.5 5.9 %collective-permute-done.13 = f32[128,33]{0,1:T(8,128)S(1)} collective-permute-done((f32[128,33]{0,1:T(8,128)S(1)}, f32[128,33]{0,1:T(8,128)S(1)}, u32[]{:S(2)}, u32[]{:S(2)}) %collective-permute-start.13) | collective-permute-done | bytes 16928 | tf_op jit(solution)/shard_map/ppermute | solution.py:50
  211.4 5.9 %collective-permute-done.14 = f32[128,33]{0,1:T(8,128)S(1)} collective-permute-done((f32[128,33]{0,1:T(8,128)S(1)}, f32[128,33]{0,1:T(8,128)S(1)}, u32[]{:S(2)}, u32[]{:S(2)}) %collective-permute-start.14) | collective-permute-done | bytes 16928 | tf_op jit(solution)/shard_map/ppermute | solution.py:50
  217.5 11.3 %fusion.18 = f32[16,33,1024]{2,1,0:T(8,128)S(1)} fusion(s32[1024,16,128]{2,0,1:T(8,128)} %copy.15, f32[16,128]{1,0:T(8,128)S(1)} %bitcast.30, f32[16,128]{1,0:T(8,128)S(1)} %bitcast.29, pred[16,128]{1,0:T(8,128)(4,1)S(1)} %fusion.31, f32[16,128,33]{1,0,2:T(8,128)S(1)} %slice_bitcast_fusion), kind=kOutput, calls=%fused_computation.21 | convolution fusion | flops 839401472 | bytes 10840064 | tf_op jit(solution)/shard_map/skm,kmr->krs/dot_general | solution.py:58
  233.1 60.7 %psum.7 = f32[16,16,33]{0,1,2:T(8,128)S(1)} all-reduce(f32[16,16,33]{0,1,2:T(8,128)S(1)} %convolution_bitcast_fusion), channel_id=1, replica_groups=mesh['grp'=2,'samp'=16] {'samp'}, use_global_device_ids=true, to_apply=%region_2.3 | all-reduce | flops 8448 | bytes 67584 | tf_op jit(solution)/shard_map/psum | solution.py:62
  (57 shorter events, 11.7 us)
Async XLA Ops:
  7.2 30.2 %copy-start = (f32[2048]{0:T(1024)S(1)}, f32[2048]{0:T(1024)}, u32[]{:S(2)}) copy-start(f32[2048]{0:T(1024)} %param.9) | copy-start | bytes 24580
  7.2 121.4 %reduce-scatter.2.cloned.1.call-start = ((), (), s32[]{:S(2)}) async-start(), calls=%async_computation.1 | async-start | bytes 348160 | tf_op jit(solution)/shard_map/reduce_scatter | solution.py:20
  37.4 11.8 %copy-start.1 = (f32[2048]{0:T(1024)S(1)}, f32[2048]{0:T(1024)}, u32[]{:S(2)}) copy-start(f32[2048]{0:T(1024)} %param.10) | copy-start | bytes 24580
  37.4 23.6 %copy-start.3 = (s32[32,1024]{1,0:T(8,128)S(1)}, s32[32,1024]{1,0:T(8,128)}, u32[]{:S(2)}) copy-start(s32[32,1024]{1,0:T(8,128)} %param.7) | copy-start | bytes 393220
  37.4 23.6 %copy-start.4 = (f32[1024]{0:T(1024)S(1)}, f32[1024]{0:T(1024)}, u32[]{:S(2)}) copy-start(f32[1024]{0:T(1024)} %param.8) | copy-start | bytes 12292
  128.5 6.1 %collective-permute-start = (f32[128,33]{0,1:T(8,128)}, f32[128,33]{0,1:T(8,128)S(1)}, u32[]{:S(2)}, u32[]{:S(2)}) collective-permute-start(f32[128,33]{0,1:T(8,128)} %reduce-scatter.2.cloned.1.call-done), channel_id=1, source_target_pairs={{0,1},{1,2},{2,3},{3,4},{4,5},{5,6},{6,7},{7,8},{8,9},{9,10},{10,1... | collective-permute-start | bytes 50696 | tf_op jit(solution)/shard_map/ppermute | solution.py:50
  134.6 5.9 %collective-permute-start.1 = (f32[128,33]{0,1:T(8,128)S(1)}, f32[128,33]{0,1:T(8,128)S(1)}, u32[]{:S(2)}, u32[]{:S(2)}) collective-permute-start(f32[128,33]{0,1:T(8,128)S(1)} %collective-permute-done), channel_id=1, source_target_pairs={{0,1},{1,2},{2,3},{3,4},{4,5},{5,6},{6,7},{7,8},{8,9},{9,10},{10,1... | collective-permute-start | bytes 50696 | tf_op jit(solution)/shard_map/ppermute | solution.py:50
  140.6 5.9 %collective-permute-start.2 = (f32[128,33]{0,1:T(8,128)S(1)}, f32[128,33]{0,1:T(8,128)S(1)}, u32[]{:S(2)}, u32[]{:S(2)}) collective-permute-start(f32[128,33]{0,1:T(8,128)S(1)} %collective-permute-done.1), channel_id=1, source_target_pairs={{0,1},{1,2},{2,3},{3,4},{4,5},{5,6},{6,7},{7,8},{8,9},{9,10},{10,1... | collective-permute-start | bytes 50696 | tf_op jit(solution)/shard_map/ppermute | solution.py:50
  146.5 5.9 %collective-permute-start.3 = (f32[128,33]{0,1:T(8,128)S(1)}, f32[128,33]{0,1:T(8,128)S(1)}, u32[]{:S(2)}, u32[]{:S(2)}) collective-permute-start(f32[128,33]{0,1:T(8,128)S(1)} %collective-permute-done.2), channel_id=1, source_target_pairs={{0,1},{1,2},{2,3},{3,4},{4,5},{5,6},{6,7},{7,8},{8,9},{9,10},{10,1... | collective-permute-start | bytes 50696 | tf_op jit(solution)/shard_map/ppermute | solution.py:50
  152.4 5.9 %collective-permute-start.4 = (f32[128,33]{0,1:T(8,128)S(1)}, f32[128,33]{0,1:T(8,128)S(1)}, u32[]{:S(2)}, u32[]{:S(2)}) collective-permute-start(f32[128,33]{0,1:T(8,128)S(1)} %collective-permute-done.3), channel_id=1, source_target_pairs={{0,1},{1,2},{2,3},{3,4},{4,5},{5,6},{6,7},{7,8},{8,9},{9,10},{10,1... | collective-permute-start | bytes 50696 | tf_op jit(solution)/shard_map/ppermute | solution.py:50
  158.3 5.9 %collective-permute-start.5 = (f32[128,33]{0,1:T(8,128)S(1)}, f32[128,33]{0,1:T(8,128)S(1)}, u32[]{:S(2)}, u32[]{:S(2)}) collective-permute-start(f32[128,33]{0,1:T(8,128)S(1)} %collective-permute-done.4), channel_id=1, source_target_pairs={{0,1},{1,2},{2,3},{3,4},{4,5},{5,6},{6,7},{7,8},{8,9},{9,10},{10,1... | collective-permute-start | bytes 50696 | tf_op jit(solution)/shard_map/ppermute | solution.py:50
  164.2 5.9 %collective-permute-start.6 = (f32[128,33]{0,1:T(8,128)S(1)}, f32[128,33]{0,1:T(8,128)S(1)}, u32[]{:S(2)}, u32[]{:S(2)}) collective-permute-start(f32[128,33]{0,1:T(8,128)S(1)} %collective-permute-done.5), channel_id=1, source_target_pairs={{0,1},{1,2},{2,3},{3,4},{4,5},{5,6},{6,7},{7,8},{8,9},{9,10},{10,1... | collective-permute-start | bytes 50696 | tf_op jit(solution)/shard_map/ppermute | solution.py:50
  170.1 5.9 %collective-permute-start.7 = (f32[128,33]{0,1:T(8,128)S(1)}, f32[128,33]{0,1:T(8,128)S(1)}, u32[]{:S(2)}, u32[]{:S(2)}) collective-permute-start(f32[128,33]{0,1:T(8,128)S(1)} %collective-permute-done.6), channel_id=1, source_target_pairs={{0,1},{1,2},{2,3},{3,4},{4,5},{5,6},{6,7},{7,8},{8,9},{9,10},{10,1... | collective-permute-start | bytes 50696 | tf_op jit(solution)/shard_map/ppermute | solution.py:50
  176.0 5.9 %collective-permute-start.8 = (f32[128,33]{0,1:T(8,128)S(1)}, f32[128,33]{0,1:T(8,128)S(1)}, u32[]{:S(2)}, u32[]{:S(2)}) collective-permute-start(f32[128,33]{0,1:T(8,128)S(1)} %collective-permute-done.7), channel_id=1, source_target_pairs={{0,1},{1,2},{2,3},{3,4},{4,5},{5,6},{6,7},{7,8},{8,9},{9,10},{10,1... | collective-permute-start | bytes 50696 | tf_op jit(solution)/shard_map/ppermute | solution.py:50
  181.9 5.9 %collective-permute-start.9 = (f32[128,33]{0,1:T(8,128)S(1)}, f32[128,33]{0,1:T(8,128)S(1)}, u32[]{:S(2)}, u32[]{:S(2)}) collective-permute-start(f32[128,33]{0,1:T(8,128)S(1)} %collective-permute-done.8), channel_id=1, source_target_pairs={{0,1},{1,2},{2,3},{3,4},{4,5},{5,6},{6,7},{7,8},{8,9},{9,10},{10,1... | collective-permute-start | bytes 50696 | tf_op jit(solution)/shard_map/ppermute | solution.py:50
  187.8 5.9 %collective-permute-start.10 = (f32[128,33]{0,1:T(8,128)S(1)}, f32[128,33]{0,1:T(8,128)S(1)}, u32[]{:S(2)}, u32[]{:S(2)}) collective-permute-start(f32[128,33]{0,1:T(8,128)S(1)} %collective-permute-done.9), channel_id=1, source_target_pairs={{0,1},{1,2},{2,3},{3,4},{4,5},{5,6},{6,7},{7,8},{8,9},{9,10},{10,1... | collective-permute-start | bytes 50696 | tf_op jit(solution)/shard_map/ppermute | solution.py:50
  193.7 5.9 %collective-permute-start.11 = (f32[128,33]{0,1:T(8,128)S(1)}, f32[128,33]{0,1:T(8,128)S(1)}, u32[]{:S(2)}, u32[]{:S(2)}) collective-permute-start(f32[128,33]{0,1:T(8,128)S(1)} %collective-permute-done.10), channel_id=1, source_target_pairs={{0,1},{1,2},{2,3},{3,4},{4,5},{5,6},{6,7},{7,8},{8,9},{9,10},{10,1... | collective-permute-start | bytes 50696 | tf_op jit(solution)/shard_map/ppermute | solution.py:50
  199.6 5.9 %collective-permute-start.12 = (f32[128,33]{0,1:T(8,128)S(1)}, f32[128,33]{0,1:T(8,128)S(1)}, u32[]{:S(2)}, u32[]{:S(2)}) collective-permute-start(f32[128,33]{0,1:T(8,128)S(1)} %collective-permute-done.11), channel_id=1, source_target_pairs={{0,1},{1,2},{2,3},{3,4},{4,5},{5,6},{6,7},{7,8},{8,9},{9,10},{10,1... | collective-permute-start | bytes 50696 | tf_op jit(solution)/shard_map/ppermute | solution.py:50
  205.5 5.9 %collective-permute-start.13 = (f32[128,33]{0,1:T(8,128)S(1)}, f32[128,33]{0,1:T(8,128)S(1)}, u32[]{:S(2)}, u32[]{:S(2)}) collective-permute-start(f32[128,33]{0,1:T(8,128)S(1)} %collective-permute-done.12), channel_id=1, source_target_pairs={{0,1},{1,2},{2,3},{3,4},{4,5},{5,6},{6,7},{7,8},{8,9},{9,10},{10,1... | collective-permute-start | bytes 50696 | tf_op jit(solution)/shard_map/ppermute | solution.py:50
  211.4 5.9 %collective-permute-start.14 = (f32[128,33]{0,1:T(8,128)S(1)}, f32[128,33]{0,1:T(8,128)S(1)}, u32[]{:S(2)}, u32[]{:S(2)}) collective-permute-start(f32[128,33]{0,1:T(8,128)S(1)} %collective-permute-done.13), channel_id=1, source_target_pairs={{0,1},{1,2},{2,3},{3,4},{4,5},{5,6},{6,7},{7,8},{8,9},{9,10},{10,1... | collective-permute-start | bytes 50696 | tf_op jit(solution)/shard_map/ppermute | solution.py:50
  230.0 64.7 %copy-start.2 = (f32[16,33,1024]{2,0,1:T(8,128)}, f32[16,33,1024]{2,0,1:T(8,128)S(1)}, u32[]{:S(2)}) copy-start(f32[16,33,1024]{2,0,1:T(8,128)S(1)} %copy.19) | copy-start | bytes 6488068
Sparse Core Ops, SparseCore 0:
  73.5 55.0 reduce-scatter.1
